TPU v7x, 512 devices: a whole 4x8x8 slice. The times are simulated.
512 devices in a mesh: ka: 8 (over y_hi, core), pb: 16 (over y_lo, z), row: 4 (over x).
Axes of the slice: x: 4, y: 8 (y_hi: 4, y_lo: 2; y = y_hi * 2 + y_lo), z: 8, core: 2. Of those that a mesh axis runs over, the one named last changes fastest.
Arguments:
- coupling: bfloat16 [64, 64, 20736], P('pb', ('ka', 'row')), may hold values from -1 to 1
- rotation: bfloat16 [64, 36, 36], P('pb'), may hold values from -1 to 1
- freq: float32 [64, 36], P('pb'), may hold values from 0.02 to 0.3
- eigvec: bfloat16 [1024, 24, 24], P(('ka', 'row')), may hold values from -1.25 to 1.25
- energies: float32 [1024, 24], P(('ka', 'row')), may hold values from -1.5 to 1.5
- window: int32 [1024], P(('ka', 'row')), may hold values from 12 to 24
- kq_index: int32 [64, 1024], P('pb'), may hold values from 0 to 1023, as said below
- kpoints: float32 [1024, 3], replicated, may hold values from 0 to 1
- lattice: int32 [64, 3], replicated, may hold values from -3 to 3
Outputs:
- electron: float32 [1024, 24], P(('ka', 'row'))
- phonon: float32 [64, 36], P('pb')
Inputs may be any that keep to these rules, and one draw needn't show every extreme that they name: The k-points form a shifted grid of 1024 points, (1024 // 64) x 8 x 8, listed in an order drawn from the seed; each q-point is a vector of that grid without the shift. kq_index[q, k] is the index of the k-point equal to kpoints[k] plus the q-point's vector modulo 1, so each row of kq_index is a permutation of 0 to 1023.
All inputs are finite; a program needn't handle non-finite values.
Results may differ from a plain program's by a relative error of at most 0.00089.
Values may be sent and summed in bfloat16 or wider, within the bound.
A program may use at most 128 MiB of HBM per device.

v0:
```python
import math
import jax
import jax.numpy as jnp
from jax import lax
from jax.sharding import PartitionSpec as P

SIGMA = 0.1
THERMAL_ENERGY_KT = 0.2


def phase_table(lattice, kpoint_rows):
    rvec = lattice.astype(jnp.float32)
    argument = (
        rvec[:, 0:1] * kpoint_rows[:, 0][None, :]
        + rvec[:, 1:2] * kpoint_rows[:, 1][None, :]
        + rvec[:, 2:3] * kpoint_rows[:, 2][None, :]
    )
    return jnp.cos(2.0 * math.pi * argument).astype(jnp.bfloat16)


def block_terms(
    coup_rows, phase_cols, rot_rows, freq_rows, eig_k, eig_kq, level_k, level_kq, lim_k, lim_kq
):
    q_block = coup_rows.shape[0]
    k_block = phase_cols.shape[1]
    columns = q_block * k_block
    n_modes = rot_rows.shape[1]
    n_bands = eig_k.shape[0]
    norm = 1.0 / (math.sqrt(2.0 * math.pi) * SIGMA)
    bloch = jnp.einsum(
        "qrf,rk->fqk", coup_rows, phase_cols, preferred_element_type=jnp.float32
    ).astype(jnp.bfloat16)
    bloch = bloch.reshape(n_modes, n_bands, n_bands, columns)
    rot_cols = jnp.repeat(jnp.transpose(rot_rows, (1, 2, 0)), k_block, axis=2)
    modal = jnp.einsum(
        "amnc,abc->bmnc", bloch, rot_cols, preferred_element_type=jnp.float32
    ).astype(jnp.bfloat16)
    eig_k_cols = jnp.tile(eig_k, (1, 1, q_block))
    right = jnp.einsum(
        "bmjc,jnc->bmnc", modal, eig_k_cols, preferred_element_type=jnp.float32
    ).astype(jnp.bfloat16)
    coupled = jnp.einsum("imc,binc->bmnc", eig_kq, right, preferred_element_type=jnp.float32)
    level_k_cols = jnp.tile(level_k, (1, q_block))
    lim_k_cols = jnp.tile(lim_k, (q_block,))
    freq_cols = jnp.repeat(freq_rows.T, k_block, axis=1)
    diff = level_kq[None, :, None, :] - level_k_cols[None, None, :, :] - freq_cols[:, None, None, :]
    delta = jnp.exp(-(diff * diff) / (2.0 * SIGMA * SIGMA)) * norm
    bands = jnp.arange(n_bands).astype(jnp.float32)
    mask_m = (bands[:, None] < lim_kq[None, :]).astype(jnp.float32)
    mask_n = (bands[:, None] < lim_k_cols[None, :]).astype(jnp.float32)
    strength = coupled * coupled * delta * mask_m[None, :, None, :] * mask_n[None, None, :, :]
    filling_initial = jax.nn.sigmoid(-level_k_cols / THERMAL_ENERGY_KT)
    filling_final = jax.nn.sigmoid(-level_kq / THERMAL_ENERGY_KT)
    elec = jnp.sum(strength, axis=(0, 1)).reshape(n_bands, q_block, k_block).sum(axis=1)
    phon = jnp.sum(
        strength * (filling_initial[None, None, :, :] - filling_final[None, :, None, :]),
        axis=(1, 2),
    )
    phon = phon.reshape(n_modes, q_block, k_block).sum(axis=2)
    return (elec, phon)


def on_device(coupling, rotation, freq, eigvec, energies, window, kq_index, kpoints, lattice):
    n_ka = lax.axis_size("ka")
    n_row = lax.axis_size("row")
    n_pb = lax.axis_size("pb")
    k_dev = eigvec.shape[0]
    q_dev = rotation.shape[0]
    n_bands = eigvec.shape[1]
    n_modes = rotation.shape[1]
    total_k = k_dev * n_ka * n_row
    total_q = q_dev * n_pb
    eigen_grid = lax.all_gather(eigvec, ("ka", "row"), axis=0, tiled=True)
    level_all, limit_all = (
        lax.all_gather(energies, ("ka", "row"), axis=0, tiled=True),
        lax.all_gather(window.astype(jnp.float32), ("ka", "row"), axis=0, tiled=True),
    )
    eig_cols = jnp.transpose(eigen_grid, (1, 2, 0))
    level_cols = level_all.T
    ka_pos = lax.axis_index("ka")
    row_pos = lax.axis_index("row")
    coup_full = lax.all_gather(coupling, ("ka", "row"), axis=1, tiled=True)
    q_start = jnp.int32(0)
    k_start = (ka_pos * n_row + row_pos) * k_dev
    kq_mine = lax.dynamic_slice(kq_index, (q_start, k_start), (q_dev, k_dev))
    kp_mine = lax.dynamic_slice(kpoints, (k_start, jnp.int32(0)), (k_dev, 3))
    eig_mine = lax.dynamic_slice_in_dim(eig_cols, k_start, k_dev, 2)
    lev_mine = lax.dynamic_slice_in_dim(level_cols, k_start, k_dev, 1)
    lim_mine = lax.dynamic_slice_in_dim(limit_all, k_start, k_dev, 0)
    phase_all = phase_table(lattice, kp_mine)
    k_block = min(k_dev, 128)
    elec_cols = [None] * (k_dev // k_block)
    index = kq_mine.reshape(-1)
    eig_kq = jnp.take(eig_cols, index, axis=2)
    level_kq = jnp.take(level_cols, index, axis=1)
    lim_kq = jnp.take(limit_all, index, axis=0)
    elec, phon = block_terms(
        coup_full, phase_all, rotation, freq, eig_mine, eig_kq, lev_mine, level_kq, lim_mine, lim_kq
    )
    elec_cols[0] = elec
    elec_local = elec_cols[0].T * (1.0 / (total_q * n_modes * n_bands))
    phon_local = phon.T * (1.0 / (total_k * n_bands))
    phonon = lax.psum(phon_local, ("ka", "row"))
    electron = lax.psum(elec_local, "pb")
    return (electron, phonon)


def solution(mesh):
    return jax.shard_map(
        on_device,
        mesh=mesh,
        in_specs=(
            P("pb", ("ka", "row"), None),
            P("pb", None, None),
            P("pb", None),
            P(("ka", "row"), None, None),
            P(("ka", "row"), None),
            P(("ka", "row")),
            P("pb", None),
            P(),
            P(),
        ),
        out_specs=(P(("ka", "row"), None), P("pb", None)),
        check_vma=False,
    )
```

profile of v0, /device:TPU:40, one launch (start us, length us, event | category | flops | bytes accessed | tf_op | source)
XLA Modules:
  0.0 554.0 jit_solution(66930285304489676)
XLA Ops:
  7.2 0.0 copy-start
  7.2 0.0 all-gather.4.cloned.1.call-start
  7.2 1.7 copy.47
  9.0 0.0 all-gather.4.cloned.1.call-update
  9.0 0.0 all-gather.6.cloned.1.call-start
  9.0 1.8 copy.49
  10.9 0.0 all-gather.6.cloned.1.call-update
  10.9 0.0 copy-done
  10.9 0.1 constant_dynamic-slice_fusion
  11.0 0.1 reshape.215
  11.1 0.1 reshape.214
  11.2 0.7 convert_element_type.50
  11.8 1.3 dynamic-slice.8
  13.8 0.8 convert_dynamic-update-slice_fusion
  14.5 78.9 %all-reduce = f32[1024]{0:T(1024)S(1)} all-reduce(f32[1024]{0:T(1024)S(1)} %convert_dynamic-update-slice_fusion), channel_id=1, replica_groups=mesh['ka'=8,'pb'=16,'row'=4] {'ka','row'}, use_global_device_ids=true, to_apply=%add | all-reduce | flops 1024 | bytes 8192
  93.5 0.1 dynamic_slice.19
  93.6 1.0 gather_fusion.2
  94.6 0.1 lt.84
  94.6 0.8 copy.79
  95.4 0.1 compare_convert_fusion.1
  95.5 0.1 copy.62
  95.6 0.1 copy.63
  95.7 82.7 %all-gather = f32[32,32,24]{1,2,0:T(8,128)S(1)} all-gather(f32[1,32,24]{1,2,0:T(8,128)} %bitcast.93), channel_id=1, replica_groups=mesh['ka'=8,'pb'=16,'row'=4] {'ka','row'}, dimensions={0}, use_global_device_ids=true | all-gather | bytes 101376 | tf_op jit(solution)/shard_map/all_gather | solution.py:75
  178.4 0.2 copy.57
  178.6 0.1 copy.60
  178.7 0.1 tile.13
  178.8 0.1 copy.61
  178.9 0.1 copy.64
  179.0 0.7 gather_fusion.1
  179.7 0.1 copy.58
  179.8 0.1 copy.65
  179.9 0.1 copy.59
  180.0 0.8 constant_dynamic-slice_fusion.1
  180.8 2.2 broadcast_subtract_fusion
  182.9 0.0 all-gather.4.cloned.1.call-done
  182.9 0.9 dynamic-slice_bitcast_fusion
  183.9 0.1 copy.48
  184.0 3.5 gather_fusion
  187.5 0.0 all-gather.6.cloned.1.call-done
  187.6 8.0 %fusion.4 = bf16[20736,4,32]{0,2,1:T(8,128)(2,1)} fusion(bf16[4,64,20736]{2,0,1:T(4,128)(2,1)} %all-gather.6.cloned.1.call-done, f32[32]{0:T(128)S(1)} %get-tuple-element.18, f32[64]{0:T(128)S(1)} %get-tuple-element.15, f32[32]{0:T(128)S(1)} %get-tuple-element.19, f32[64]{0:T(128)S(1)} %get-tuple-element.16, f32[32]{0:T(128)S(1)} %get-tuple-element.17, ...), kind=kOutput, calls=%fused_computation.10 | convolution fusion | flops 342407168 | bytes 15926400 | tf_op jit(solution)/shard_map/qrf,rk->fqk/dot_general | solution.py:30
  195.6 47.2 %reshape.253 = bf16[36,24,24,128]{2,1,0,3:T(8,128)(2,1)} reshape(bf16[20736,4,32]{0,2,1:T(8,128)(2,1)} %fusion.4) | data formatting | bytes 10616832 | tf_op jit(solution)/shard_map/reshape | solution.py:33
  242.8 0.1 tile.10
  242.9 0.2 broadcast_in_dim.40.clone
  243.1 0.0 copy-start.2
  243.1 23.0 %convert_bitcast_fusion = bf16[36,24,24,128]{0,2,1,3:T(8,128)(2,1)} fusion(bf16[24,24,128,1]{0,1,3,2:T(8,128)(2,1)S(1)} %bitcast.86, bf16[36,36,128,1]{1,0,3,2:T(8,128)(2,1)S(1)} %bitcast.85, bf16[36,24,24,128]{2,1,0,3:T(8,128)(2,1)} %reshape.253), kind=kOutput, calls=%fused_computation.15 | convolution fusion | flops 323813376 | bytes 11096064 | tf_op jit(solution)/shard_map/bmjc,jnc->bmnc/dot_general | solution.py:39
  266.1 0.0 copy-done.2
  266.1 0.0 copy-start.1
  266.1 69.3 %multiply_reduce_fusion = (f32[36,128]{0,1:T(8,128)S(1)}, f32[24,128]{0,1:T(8,128)S(1)}) fusion(f32[24,24,128]{0,1,2:T(8,128)} %get-tuple-element.22, f32[24,128]{0,1:T(8,128)S(1)} %copy.63, f32[24,128]{0,1:T(8,128)S(1)} %copy.62, f32[36,128]{0,1:T(8,128)S(1)} %bitcast.90, f32[24,24,128]{0,1,2:T(8,128)} %get-tuple-element.23, ...), kind=kOutput, calls=%fused_computation.6 | convolution fusion | flops 159318528 | bytes 6119552 | tf_op jit(solution)/shard_map/imc,binc->bmnc/dot_general | solution.py:42
  335.5 69.8 %psum.14 = f32[32,24]{1,0:T(8,128)S(1)} all-reduce(f32[32,24]{1,0:T(8,128)S(1)} %multiply_bitcast_fusion.1), channel_id=1, replica_groups=mesh['ka'=8,'pb'=16,'row'=4] {'pb'}, use_global_device_ids=true, to_apply=%region_2.3 | all-reduce | flops 768 | bytes 6144 | tf_op jit(solution)/shard_map/psum | solution.py:104
  405.3 0.7 copy.67
  405.9 0.1 copy.78
  406.0 140.5 %psum.15 = f32[4,36]{0,1:T(8,128)S(1)} all-reduce(f32[4,36]{0,1:T(8,128)S(1)} %multiply_bitcast_fusion), channel_id=1, replica_groups=mesh['ka'=8,'pb'=16,'row'=4] {'ka','row'}, use_global_device_ids=true, to_apply=%region_5.6 | all-reduce | flops 144 | bytes 1152 | tf_op jit(solution)/shard_map/psum | solution.py:103
  546.5 0.7 copy.68
  547.2 0.0 copy-done.1
  (17 shorter events, 0.2 us)
Async XLA Ops:
  7.2 3.7 copy-start
  7.2 175.7 %all-gather.4.cloned.1.call-start = ((), (), s32[]{:S(2)}) async-start(), calls=%async_computation | async-start | bytes 6488064 | tf_op jit(solution)/shard_map/all_gather | solution.py:73
  9.0 178.6 %all-gather.6.cloned.1.call-start = ((), (), s32[]{:S(2)}) async-start(), calls=%async_computation.1 | async-start | bytes 10948608 | tf_op jit(solution)/shard_map/all_gather | solution.py:82
  243.1 23.0 %copy-start.2 = (f32[4,36]{1,0:T(4,128)S(1)}, f32[4,36]{1,0:T(4,128)}, u32[]{:S(2)}) copy-start(f32[4,36]{1,0:T(4,128)} %param.11) | copy-start | bytes 1732
  266.1 281.1 %copy-start.1 = (s32[4,1024]{1,0:T(4,128)S(1)}, s32[4,1024]{1,0:T(4,128)}, u32[]{:S(2)}) copy-start(s32[4,1024]{1,0:T(4,128)} %param.15) | copy-start | bytes 49156
Sparse Core Ops, SparseCore 0:
  11.1 75.5 all-gather.3
  89.9 93.6 all-gather.5
where the time goes:
time: 555 us; the launch traced here: 554 us
  blocking collectives  372 us (67%)
  matrix products  100 us (18%)
  local copies, waits for them, and re-layouts  63 us (11%)
  between operations  14.9 us (3%)
    psum x1, blocking collectives, on_device(): phonon = lax.psum(phon_local, ('ka', 'row'))  140 us
    all_gather x1, blocking collectives, on_device(): lax.all_gather(energies, ('ka', 'row'), axis=0, tiled=True)  82.7 us
    unnamed x1, blocking collectives  78.9 us
    psum x1, blocking collectives, on_device(): electron = lax.psum(elec_local, 'pb')  69.8 us
    dot_general x1, matrix products, block_terms(): jnp.einsum('imc,binc->bmnc', eig_kq, right, preferred_element_type=jnp.fl...  69.3 us
    reshape x1, local copies, waits for them, and re-layouts, block_terms(): bloch = bloch.reshape(n_modes, n_bands, n_bands, columns)  47.2 us
    dot_general x1, matrix products, block_terms(): jnp.einsum('bmjc,jnc->bmnc', modal, eig_k_cols, preferred_element_type=jn...  23 us
  transfers between devices with their start and end apart: 2, of which 0 were waited for; matrix products, arithmetic and copies ran while one was open for 3% of the time, Pallas kernels for 0%

commit v1 on v0

--- a/solution.py
+++ b/solution.py
@@ -1,3 +1,4 @@
+import functools
 import math
 import jax
 import jax.numpy as jnp
@@ -6,6 +7,15 @@
 
 SIGMA = 0.1
 THERMAL_ENERGY_KT = 0.2
+
+
+def pass_cube(base_x, lane_axis, net_axis):
+    for tick in (lane_axis, net_axis):
+        base_x = lax.psum(base_x, axis_name=tick)
+    return base_x
+
+
+advance_desk = functools.partial(pass_cube, lane_axis="ka", net_axis="row")
 
 
 def phase_table(lattice, kpoint_rows):
@@ -100,7 +110,7 @@
     elec_cols[0] = elec
     elec_local = elec_cols[0].T * (1.0 / (total_q * n_modes * n_bands))
     phon_local = phon.T * (1.0 / (total_k * n_bands))
-    phonon = lax.psum(phon_local, ("ka", "row"))
+    phonon = advance_desk(phon_local)
     electron = lax.psum(elec_local, "pb")
     return (electron, phonon)
 

time: 555 us -> 458 us (0.83)
  blocking collectives: 372 us -> 275 us
    psum x1 -> x2, blocking collectives: 140 us -> 43.7 us  [pass_cube(): base_x = lax.psum(base_x, axis_name=tick)]
  transfers between devices with their start and end apart: 2 -> 2, of which waited for: 0 -> 0; matrix products, arithmetic and copies ran while one was open for 3% -> 4% of each run, Pallas kernels for 0% -> 0%
where the time goes in v1:
time: 458 us; the launch traced here: 457 us
  blocking collectives  275 us (60%)
  matrix products  100 us (22%)
  local copies, waits for them, and re-layouts  63.1 us (14%)
  between operations  14.9 us (3%)
    all_gather x1, blocking collectives, on_device(): lax.all_gather(energies, ('ka', 'row'), axis=0, tiled=True)  82.7 us
    unnamed x1, blocking collectives  78.9 us
    psum x1, blocking collectives, on_device(): electron = lax.psum(elec_local, 'pb')  69.8 us
    dot_general x1, matrix products, block_terms(): jnp.einsum('imc,binc->bmnc', eig_kq, right, preferred_element_type=jnp.fl...  69.3 us
    reshape x1, local copies, waits for them, and re-layouts, block_terms(): bloch = bloch.reshape(n_modes, n_bands, n_bands, columns)  47.2 us
    psum x2, blocking collectives, pass_cube(): base_x = lax.psum(base_x, axis_name=tick)  43.7 us
    dot_general x1, matrix products, block_terms(): jnp.einsum('bmjc,jnc->bmnc', modal, eig_k_cols, preferred_element_type=jn...  23 us
  transfers between devices with their start and end apart: 2, of which 0 were waited for; matrix products, arithmetic and copies ran while one was open for 4% of the time, Pallas kernels for 0%

profile of v1, /device:TPU:40, one launch (start us, length us, event | category | flops | bytes accessed | tf_op | source)
XLA Modules:
  0.0 457.2 jit_solution(8716118293926351780)
XLA Ops:
  7.2 0.0 copy-start
  7.2 0.0 all-gather.4.cloned.1.call-start
  7.2 1.7 copy.47
  9.0 0.0 all-gather.4.cloned.1.call-update
  9.0 0.0 all-gather.6.cloned.1.call-start
  9.0 1.8 copy.49
  10.9 0.0 all-gather.6.cloned.1.call-update
  10.9 0.0 copy-done
  10.9 0.1 constant_dynamic-slice_fusion
  11.0 0.1 reshape.215
  11.1 0.1 reshape.214
  11.2 0.7 convert_element_type.50
  11.8 1.3 dynamic-slice.8
  13.8 0.8 convert_dynamic-update-slice_fusion
  14.5 78.9 %all-reduce = f32[1024]{0:T(1024)S(1)} all-reduce(f32[1024]{0:T(1024)S(1)} %convert_dynamic-update-slice_fusion), channel_id=1, replica_groups=mesh['ka'=8,'pb'=16,'row'=4] {'ka','row'}, use_global_device_ids=true, to_apply=%add | all-reduce | flops 1024 | bytes 8192
  93.5 0.1 dynamic_slice.19
  93.6 1.0 gather_fusion.2
  94.6 0.1 lt.84
  94.6 0.8 copy.79
  95.4 0.1 compare_convert_fusion.1
  95.5 0.1 copy.62
  95.6 0.1 copy.63
  95.7 82.7 %all-gather = f32[32,32,24]{1,2,0:T(8,128)S(1)} all-gather(f32[1,32,24]{1,2,0:T(8,128)} %bitcast.93), channel_id=1, replica_groups=mesh['ka'=8,'pb'=16,'row'=4] {'ka','row'}, dimensions={0}, use_global_device_ids=true | all-gather | bytes 101376 | tf_op jit(solution)/shard_map/all_gather | solution.py:85
  178.4 0.2 copy.57
  178.6 0.1 copy.60
  178.7 0.1 tile.13
  178.8 0.1 copy.61
  178.9 0.1 copy.64
  179.0 0.7 gather_fusion.1
  179.7 0.1 copy.58
  179.8 0.1 copy.65
  179.9 0.1 copy.59
  180.0 0.8 constant_dynamic-slice_fusion.1
  180.8 2.2 broadcast_subtract_fusion
  182.9 0.0 all-gather.4.cloned.1.call-done
  182.9 0.9 dynamic-slice_bitcast_fusion
  183.9 0.1 copy.48
  184.0 3.5 gather_fusion
  187.5 0.0 all-gather.6.cloned.1.call-done
  187.6 8.0 %fusion.4 = bf16[20736,4,32]{0,2,1:T(8,128)(2,1)} fusion(bf16[4,64,20736]{2,0,1:T(4,128)(2,1)} %all-gather.6.cloned.1.call-done, f32[32]{0:T(128)S(1)} %get-tuple-element.18, f32[64]{0:T(128)S(1)} %get-tuple-element.15, f32[32]{0:T(128)S(1)} %get-tuple-element.19, f32[64]{0:T(128)S(1)} %get-tuple-element.16, f32[32]{0:T(128)S(1)} %get-tuple-element.17, ...), kind=kOutput, calls=%fused_computation.10 | convolution fusion | flops 342407168 | bytes 15926400 | tf_op jit(solution)/shard_map/qrf,rk->fqk/dot_general | solution.py:40
  195.6 47.2 %reshape.253 = bf16[36,24,24,128]{2,1,0,3:T(8,128)(2,1)} reshape(bf16[20736,4,32]{0,2,1:T(8,128)(2,1)} %fusion.4) | data formatting | bytes 10616832 | tf_op jit(solution)/shard_map/reshape | solution.py:43
  242.8 0.1 tile.10
  242.9 0.2 broadcast_in_dim.40.clone
  243.1 0.0 copy-start.2
  243.1 23.0 %convert_bitcast_fusion = bf16[36,24,24,128]{0,2,1,3:T(8,128)(2,1)} fusion(bf16[24,24,128,1]{0,1,3,2:T(8,128)(2,1)S(1)} %bitcast.86, bf16[36,36,128,1]{1,0,3,2:T(8,128)(2,1)S(1)} %bitcast.85, bf16[36,24,24,128]{2,1,0,3:T(8,128)(2,1)} %reshape.253), kind=kOutput, calls=%fused_computation.15 | convolution fusion | flops 323813376 | bytes 11096064 | tf_op jit(solution)/shard_map/bmjc,jnc->bmnc/dot_general | solution.py:49
  266.1 0.0 copy-done.2
  266.1 0.0 copy-start.1
  266.1 69.3 %multiply_reduce_fusion = (f32[36,128]{0,1:T(8,128)S(1)}, f32[24,128]{0,1:T(8,128)S(1)}) fusion(f32[24,24,128]{0,1,2:T(8,128)} %get-tuple-element.22, f32[24,128]{0,1:T(8,128)S(1)} %copy.63, f32[24,128]{0,1:T(8,128)S(1)} %copy.62, f32[36,128]{0,1:T(8,128)S(1)} %bitcast.90, f32[24,24,128]{0,1,2:T(8,128)} %get-tuple-element.23, ...), kind=kOutput, calls=%fused_computation.6 | convolution fusion | flops 159318528 | bytes 6119552 | tf_op jit(solution)/shard_map/imc,binc->bmnc/dot_general | solution.py:52
  335.5 69.8 %psum.21 = f32[32,24]{1,0:T(8,128)S(1)} all-reduce(f32[32,24]{1,0:T(8,128)S(1)} %multiply_bitcast_fusion.1), channel_id=1, replica_groups=mesh['ka'=8,'pb'=16,'row'=4] {'pb'}, use_global_device_ids=true, to_apply=%region_2.3 | all-reduce | flops 768 | bytes 6144 | tf_op jit(solution)/shard_map/psum | solution.py:114
  405.3 0.7 copy.67
  405.9 0.1 copy.78
  406.0 27.2 %psum.22 = f32[4,36]{0,1:T(8,128)S(1)} all-reduce(f32[4,36]{0,1:T(8,128)S(1)} %multiply_bitcast_fusion), channel_id=1, replica_groups=mesh['ka'=8,'pb'=16,'row'=4] {'ka'}, use_global_device_ids=true, to_apply=%region_5.6 | all-reduce | flops 144 | bytes 1152 | tf_op jit(solution)/shard_map/psum | solution.py:14
  433.2 16.5 %psum.23 = f32[4,36]{0,1:T(8,128)S(1)} all-reduce(f32[4,36]{0,1:T(8,128)S(1)} %psum.22), channel_id=1, replica_groups=mesh['ka'=8,'pb'=16,'row'=4] {'row'}, use_global_device_ids=true, to_apply=%region_6.7 | all-reduce | flops 144 | bytes 1152 | tf_op jit(solution)/shard_map/psum | solution.py:14
  449.7 0.7 copy.68
  450.4 0.0 copy-done.1
  (17 shorter events, 0.2 us)
Async XLA Ops:
  7.2 3.7 copy-start
  7.2 175.7 %all-gather.4.cloned.1.call-start = ((), (), s32[]{:S(2)}) async-start(), calls=%async_computation | async-start | bytes 6488064 | tf_op jit(solution)/shard_map/all_gather | solution.py:83
  9.0 178.6 %all-gather.6.cloned.1.call-start = ((), (), s32[]{:S(2)}) async-start(), calls=%async_computation.1 | async-start | bytes 10948608 | tf_op jit(solution)/shard_map/all_gather | solution.py:92
  243.1 23.0 %copy-start.2 = (f32[4,36]{1,0:T(4,128)S(1)}, f32[4,36]{1,0:T(4,128)}, u32[]{:S(2)}) copy-start(f32[4,36]{1,0:T(4,128)} %param.11) | copy-start | bytes 1732
  266.1 184.3 %copy-start.1 = (s32[4,1024]{1,0:T(4,128)S(1)}, s32[4,1024]{1,0:T(4,128)}, u32[]{:S(2)}) copy-start(s32[4,1024]{1,0:T(4,128)} %param.15) | copy-start | bytes 49156
Sparse Core Ops, SparseCore 0:
  11.1 75.5 all-gather.3
  89.9 93.6 all-gather.5
